TPU v7x, 32 devices: a whole 2x2x4 slice. The times are simulated.
32 devices in a mesh: les: 8 (over y, x, core), modes: 4 (over z).
Axes of the slice: x: 2, y: 2, z: 4, core: 2. Of those that a mesh axis runs over, the one named last changes fastest.
Arguments:
- pressure: bfloat16 [65536, 512], P('les', 'modes'), may hold values from -6 to 6
- targets: int32 [65536], P('les'), may hold values from 0 to 32767, as said below
- counts: int32 [8], P('les'), may hold values from 1 to 8192, as said below
- pseudo_inverse: bfloat16 [2, 1536, 16384], P(None, None, ('les', 'modes')), may hold values from -0.046875 to 0.046875
Outputs:
- harmonics: float32 [2, 2, 8, 1536], P(None, None, None, ('les', 'modes'))
Inputs may be any that keep to these rules, and one draw needn't show every extreme that they name: `counts`: some partition holds exactly 8192 live faces; all partitions together hold 32768. `targets`: the live slots (slot f of partition i with f < counts[i]) name every station point exactly once. Point p of a station lies in the point rows of les index p // (512 * 4); at most 1024 live faces of one partition lie in the point rows of one les index, and some partition reaches that bound. Slots that are not live hold arbitrary indices in the range.
All inputs are finite; a program needn't handle non-finite values.
Results may differ from a plain program's by a relative error of at most 0.0003.
Values may be sent and summed in bfloat16 or wider, within the bound.
A program may use at most 64 MiB of HBM per device.

v0:
```python
import math
import jax
import jax.numpy as jnp
from jax import lax
from jax.sharding import PartitionSpec as P

TIME = 512
HARM = 8


def fourier_rows():
    sample_ids = jnp.arange(TIME, dtype=jnp.int32)
    orders = jnp.arange(1, HARM + 1, dtype=jnp.int32)
    phase_ids = orders[:, None] * sample_ids[None, :] % TIME
    angles = phase_ids.astype(jnp.float32) * (2.0 * math.pi / TIME)
    scale_factor = math.sqrt(2.0 / TIME)
    return jnp.stack([jnp.cos(angles), -jnp.sin(angles)]) * scale_factor


def rank_by_owner(dest_les, is_live, les_count):
    face_slots = dest_les.shape[0]
    span_width = math.gcd(face_slots, 128)
    owner_ids = jnp.arange(les_count, dtype=jnp.int32)
    matches = ((dest_les[None, :] == owner_ids[:, None]) & is_live[None, :]).astype(jnp.float32)
    matches = matches.reshape(les_count, face_slots // span_width, span_width)
    position = jnp.arange(span_width, dtype=jnp.int32)
    upper = (position[:, None] <= position[None, :]).astype(jnp.float32)
    within = jnp.einsum("nbj,jw->nbw", matches, upper, precision=lax.Precision.HIGHEST)
    block_sums = jnp.sum(matches, axis=2)
    before = jnp.cumsum(block_sums, axis=1) - block_sums
    running = within + before[:, :, None]
    ranked = jnp.sum(running * matches, axis=0).reshape(face_slots) - 1.0
    return ranked.astype(jnp.int32)


def local(pressure, targets, counts, pseudo_inverse):
    les_count = lax.axis_size("les")
    mode_count = lax.axis_size("modes")
    block_len = pressure.shape[1]
    face_slots = targets.shape[0]
    stations = pseudo_inverse.shape[0]
    mode_total = pseudo_inverse.shape[1]
    point_dev = pseudo_inverse.shape[2]
    rows_les = point_dev * mode_count
    points_all = rows_les * les_count
    send_cap = face_slots // les_count
    send_total = les_count * send_cap
    slot_ids = jnp.arange(face_slots, dtype=jnp.int32)
    is_live = slot_ids < counts[0]
    station_of = targets // points_all
    point_of = targets % points_all
    dest_les = point_of // rows_les
    local_row = station_of * rows_les + point_of % rows_les
    face_rank = rank_by_owner(dest_les, is_live, les_count)
    send_pos = jnp.where(is_live, dest_les * send_cap + face_rank, send_total)
    source_face = jnp.full((send_total,), -1, jnp.int32).at[send_pos].set(slot_ids, mode="drop")
    slot_used = source_face >= 0
    source_safe = jnp.maximum(source_face, 0)
    row_tags = jnp.where(slot_used, jnp.take(local_row, source_safe, axis=0), -1).reshape(
        1, send_total
    )
    tags_in = lax.all_to_all(row_tags, "les", split_axis=1, concat_axis=1, tiled=True)
    arrival = jnp.where(tags_in[0] >= 0, tags_in[0], stations * rows_les)
    arrival_ids = jnp.arange(send_total, dtype=jnp.int32)
    arrived_from = (
        jnp.zeros((stations * rows_les,), jnp.int32).at[arrival].set(arrival_ids, mode="drop")
    )
    fourier = fourier_rows()
    block_start = lax.axis_index("modes") * block_len
    block_rows = lax.dynamic_slice_in_dim(fourier, block_start, block_len, 2)
    block_rows = block_rows.reshape(2 * HARM, block_len)
    spectra = lax.dot_general(
        pressure.astype(jnp.float32),
        block_rows,
        (((1,), (1,)), ((), ())),
        precision=lax.Precision.HIGHEST,
    )
    picked = jnp.take(spectra, source_safe, axis=0)
    outgoing = jnp.where(slot_used[:, None], picked, jnp.zeros_like(picked))
    incoming = lax.all_to_all(outgoing, "les", split_axis=0, concat_axis=0, tiled=True)
    gathered = jnp.take(incoming, arrived_from, axis=0)
    gathered = gathered.reshape(stations, rows_les, 2 * HARM)
    summed = lax.psum_scatter(gathered, "modes", scatter_dimension=1, tiled=True)
    partial_value = []
    for station_index in range(stations):
        weights = pseudo_inverse[station_index].astype(jnp.float32)
        projected = lax.dot_general(
            summed[station_index],
            weights,
            (((0,), (1,)), ((), ())),
            precision=lax.Precision.HIGHEST,
        )
        partial_value.append(projected.reshape(2, HARM, mode_total))
    shares = jnp.stack(partial_value)
    return lax.psum_scatter(shares, ("les", "modes"), scatter_dimension=3, tiled=True)


def solution(mesh):
    placed = (P("les", "modes"), P("les"), P("les"), P(None, None, ("les", "modes")))
    return jax.shard_map(
        local,
        mesh=mesh,
        in_specs=placed,
        out_specs=P(None, None, None, ("les", "modes")),
        check_vma=False,
    )
```

profile of v0, /device:TPU:0, one launch (start us, length us, event | category | flops | bytes accessed | tf_op | source)
XLA Modules:
  0.0 323.5 jit_solution(5124301517689672651)
XLA Ops:
  7.4 0.8 fusion.13
  8.2 0.1 convert_reduce_fusion
  8.3 0.2 reduce_window_sum.11
  8.6 0.2 fusion.5
  8.8 0.8 compare_select_fusion.2
  9.6 30.5 %scatter_custom_fusion = s32[8192]{0:T(1024)S(1)} fusion(s32[8192]{0:T(1024)S(1)} %compare_select_fusion.2, s32[8192]{0:T(1024)S(1)} %iota.64, s32[]{:T(128)} %constant.117.clone.1), kind=kCustom, calls=%fused_computation.68 | custom fusion | bytes 32772 | tf_op jit(solution)/shard_map/scatter | solution.py:56
  40.1 45.5 %gather_fusion = s32[8192]{0:T(1024)S(1)} fusion(s32[8192]{0:T(1024)S(1)} %get-tuple-element.8, s32[8192]{0:T(1024)S(1)} %maximum_clamp_fusion), kind=kCustom, calls=%fused_computation | custom fusion | bytes 98304 | tf_op jit(solution)/shard_map/jit(_take)/gather | solution.py:59
  85.6 0.6 select_select_fusion.1
  86.3 5.2 %all-to-all-start = ((s32[1,8,1024]{2,0,1:T(1,128)}), s32[1,8,1024]{2,0,1:T(1,128)S(1)}, u32[]{:S(2)}, u32[]{:S(2)}) async-start(s32[1,8,1024]{2,0,1:T(1,128)} %bitcast.4), calls=%async_computation | async-start | bytes 65536 | tf_op jit(solution)/shard_map/all_to_all | solution.py:62
  91.4 0.2 sine_negate_fusion
  91.7 1.7 convolution_bitcast_fusion
  93.4 2.6 copy.9
  96.0 29.9 %gather_fusion.1 = f32[8192,16]{1,0:T(8,128)} fusion(f32[8192,16]{1,0:T(8,128)} %copy.9, s32[8192]{0:T(1024)S(1)} %maximum_clamp_fusion), kind=kCustom, calls=%fused_computation.1 | custom fusion | bytes 1081344 | tf_op jit(solution)/shard_map/jit(_take)/gather | solution.py:78
  125.9 2.8 copy.10
  128.7 0.9 select_select_fusion
  129.6 4.2 %all-to-all-start.1 = ((f32[8,1024,16]{1,2,0:T(8,128)}), f32[8,1024,16]{1,2,0:T(8,128)S(1)}, u32[]{:S(2)}, u32[]{:S(2)}) async-start(f32[8,1024,16]{1,2,0:T(8,128)} %select_select_fusion), calls=%async_computation.1 | async-start | bytes 1048576 | tf_op jit(solution)/shard_map/all_to_all | solution.py:80
  133.8 0.0 reduce-scatter.5.cloned.1.call-start
  133.8 0.1 compare_select_fusion
  133.9 30.5 %scatter_custom_fusion.1 = s32[4096]{0:T(1024)S(1)} fusion(s32[8192]{0:T(1024)S(1)} %bitcast.62, s32[8192]{0:T(1024)S(1)} %iota.65, s32[]{:T(128)} %constant.116.clone.1), kind=kCustom, calls=%fused_computation.77 | custom fusion | bytes 16388 | tf_op jit(solution)/shard_map/scatter | solution.py:66
  164.4 2.6 copy.11
  167.0 16.3 %gather_fusion.2 = f32[4096,16]{1,0:T(8,128)} fusion(f32[8192,16]{1,0:T(8,128)} %bitcast.56, s32[4096]{0:T(1024)S(1)} %fusion.27), kind=kCustom, calls=%fused_computation.2 | custom fusion | bytes 540672 | tf_op jit(solution)/shard_map/jit(_take)/gather | solution.py:81
  183.3 2.2 copy.12
  185.4 0.7 broadcast_select_fusion
  186.2 0.0 reduce-scatter.7.cloned.1.call-start
  186.2 21.4 %reduce-scatter.5.cloned.1.call-done = f32[2,512,16]{1,2,0:T(8,128)} async-done(((f32[2,2048,16]{1,2,0:T(8,128)}), f32[2,512,16]{1,2,0:T(8,128)}) %reduce-scatter.5.cloned.1.call-update) | async-done | bytes 65552 | tf_op jit(solution)/shard_map/reduce_scatter | solution.py:83
  207.7 2.7 convolution_bitcast_fusion.1
  210.4 2.8 convolution_bitcast_fusion.2
  213.2 3.3 %copy.13 = f32[2,2,8,1536]{2,1,0,3:T(2,128)} copy(f32[2,2,8,1536]{3,2,1,0:T(8,128)S(1)} %pad_maximum_fusion) | data formatting | bytes 393216
  216.5 4.7 %reshape.276 = f32[1536,32]{1,0:T(8,128)} reshape(f32[1536,2,2,8]{3,2,1,0:T(2,128)} %bitcast.58) | data formatting | bytes 393216
  221.2 93.9 %reduce-scatter.7.cloned.1.call-done = f32[48,32]{1,0:T(8,128)} async-done(((f32[1536,32]{1,0:T(8,128)}), f32[48,32]{1,0:T(8,128)}) %reduce-scatter.7.cloned.1.call-update) | async-done | bytes 6160
  315.1 0.9 reshape.277
  315.9 0.7 copy.14
  (18 shorter events, 0.2 us)
Async XLA Ops:
  6.5 85.1 %copy-start = (bf16[8192,128]{1,0:T(8,128)(2,1)S(1)}, bf16[8192,128]{1,0:T(8,128)(2,1)}, u32[]{:S(2)}) copy-start(bf16[8192,128]{1,0:T(8,128)(2,1)} %param.4) | copy-start | bytes 6291460
  86.3 43.3 %all-to-all-start = ((s32[1,8,1024]{2,0,1:T(1,128)}), s32[1,8,1024]{2,0,1:T(1,128)S(1)}, u32[]{:S(2)}, u32[]{:S(2)}) async-start(s32[1,8,1024]{2,0,1:T(1,128)} %bitcast.4), calls=%async_computation | async-start | bytes 65536 | tf_op jit(solution)/shard_map/all_to_all | solution.py:62
  129.6 34.8 %all-to-all-start.1 = ((f32[8,1024,16]{1,2,0:T(8,128)}), f32[8,1024,16]{1,2,0:T(8,128)S(1)}, u32[]{:S(2)}, u32[]{:S(2)}) async-start(f32[8,1024,16]{1,2,0:T(8,128)} %select_select_fusion), calls=%async_computation.1 | async-start | bytes 1048576 | tf_op jit(solution)/shard_map/all_to_all | solution.py:80
  133.8 73.9 %reduce-scatter.5.cloned.1.call-start = ((), (), s32[]{:S(2)}) async-start(), calls=%async_computation.4 | async-start | bytes 327680 | tf_op jit(solution)/shard_map/reduce_scatter | solution.py:83
  186.2 128.9 %reduce-scatter.7.cloned.1.call-start = ((), (), s32[]{:S(2)}) async-start(), calls=%async_computation.5 | async-start | bytes 811008
Sparse Core Ops, SparseCore 0:
  186.3 21.3 reduce-scatter.4
  221.3 93.6 reduce-scatter.6
where the time goes:
time: 324 us; the launch traced here: 323 us
  local copies, waits for them, and re-layouts  172 us (53%)
  waiting for transfers between devices  115 us (35%)
  between operations  14.4 us (4%)
  starting transfers between devices  9.44 us (3%)
  matrix products  7.45 us (2%)
  other arithmetic  4.52 us (1%)
    unnamed x3, waiting for transfers between devices  93.9 us
    gather x1, local copies, waits for them, and re-layouts, local(): jnp.take(local_row, source_safe, axis=0)  45.5 us
    gather x2, local copies, waits for them, and re-layouts, local(): picked = jnp.take(spectra, source_safe, axis=0)  32.7 us
    scatter x1, local copies, waits for them, and re-layouts, local(): jnp.full((send_total,), -1, jnp.int32).at[send_pos]  30.5 us
    scatter x1, local copies, waits for them, and re-layouts, local(): jnp.zeros((stations * rows_les,), jnp.int32).at[arrival]  30.5 us
    reduce_scatter x1, waiting for transfers between devices, local(): lax.psum_scatter(gathered, 'modes', scatter_dimension=1, tiled=True)  21.4 us
    gather x2, local copies, waits for them, and re-layouts, local(): gathered = jnp.take(incoming, arrived_from, axis=0)  18.4 us
    unnamed x6, local copies, waits for them, and re-layouts  9.54 us
  transfers between devices with their start and end apart: 4, of which 2 were waited for; matrix products, arithmetic and copies ran while one was open for 21% of the time, Pallas kernels for 0%

commit v1 on v0

--- a/solution.py
+++ b/solution.py
@@ -6,6 +6,17 @@
 
 TIME = 512
 HARM = 8
+
+
+def in_blocks(shard, dim, size):
+    before, after = (shard.shape[:dim], shard.shape[dim + 1 :])
+    return jnp.moveaxis(shard.reshape(*before, size, -1, *after), dim, 0)
+
+
+def joined_along(blocks, dim):
+    dims = list(blocks.shape[1:])
+    dims[dim] *= blocks.shape[0]
+    return jnp.moveaxis(blocks, 0, dim).reshape(dims)
 
 
 def fourier_rows():
@@ -77,7 +88,14 @@
     )
     picked = jnp.take(spectra, source_safe, axis=0)
     outgoing = jnp.where(slot_used[:, None], picked, jnp.zeros_like(picked))
-    incoming = lax.all_to_all(outgoing, "les", split_axis=0, concat_axis=0, tiled=True)
+    length, position_2 = (lax.axis_size("les"), lax.axis_index("les"))
+    tiles = in_blocks(outgoing, 0, length)
+    finished = [tiles[position_2]]
+    for step in range(1, length):
+        sent = tiles[position_2 ^ step]
+        finished.append(lax.ppermute(sent, "les", [(i, i ^ step) for i in range(length)]))
+    tiles = jnp.stack(finished)[position_2 ^ jnp.arange(length)]
+    incoming = joined_along(tiles, 0)
     gathered = jnp.take(incoming, arrived_from, axis=0)
     gathered = gathered.reshape(stations, rows_les, 2 * HARM)
     summed = lax.psum_scatter(gathered, "modes", scatter_dimension=1, tiled=True)

time: 324 us -> 333 us (1.028)
  waiting for transfers between devices: 115 us -> 121 us
    ppermute x0 -> x7, starting transfers between devices: none -> 7.44 us  [local(): lax.ppermute(sent, 'les', [(i, i ^ step) for i in range(length)])]
    ppermute x0 -> x7, waiting for transfers between devices: none -> 6.04 us  [local(): lax.ppermute(sent, 'les', [(i, i ^ step) for i in range(length)])]
    all_to_all x1 -> x0, starting transfers between devices: 4.2 us -> none  [local(): lax.all_to_all(outgoing, 'les', split_axis=0, concat_axis=0, tiled=True)]
    unnamed x6 -> x12, local copies, waits for them, and re-layouts: 9.54 us -> 9.53 us
  transfers between devices with their start and end apart: 4 -> 10, of which waited for: 2 -> 4; matrix products, arithmetic and copies ran while one was open for 21% -> 20% of each run, Pallas kernels for 0% -> 0%
where the time goes in v1:
time: 333 us; the launch traced here: 332 us
  local copies, waits for them, and re-layouts  173 us (52%)
  waiting for transfers between devices  121 us (36%)
  between operations  14.5 us (4%)
  starting transfers between devices  12.7 us (4%)
  matrix products  7.45 us (2%)
  other arithmetic  3.74 us (1%)
    unnamed x3, waiting for transfers between devices  93.9 us
    gather x1, local copies, waits for them, and re-layouts, local(): jnp.take(local_row, source_safe, axis=0)  45.5 us
    gather x2, local copies, waits for them, and re-layouts, local(): picked = jnp.take(spectra, source_safe, axis=0)  32.7 us
    scatter x1, local copies, waits for them, and re-layouts, local(): jnp.full((send_total,), -1, jnp.int32).at[send_pos]  30.5 us
    scatter x1, local copies, waits for them, and re-layouts, local(): jnp.zeros((stations * rows_les,), jnp.int32).at[arrival]  30.5 us
    reduce_scatter x1, waiting for transfers between devices, local(): lax.psum_scatter(gathered, 'modes', scatter_dimension=1, tiled=True)  21.1 us
    gather x2, local copies, waits for them, and re-layouts, local(): gathered = jnp.take(incoming, arrived_from, axis=0)  18.4 us
    unnamed x12, local copies, waits for them, and re-layouts  9.53 us
  transfers between devices with their start and end apart: 10, of which 4 were waited for; matrix products, arithmetic and copies ran while one was open for 20% of the time, Pallas kernels for 0%

profile of v1, /device:TPU:0, one launch (start us, length us, event | category | flops | bytes accessed | tf_op | source)
XLA Modules:
  0.0 332.4 jit_solution(5239452944303648285)
XLA Ops:
  7.4 0.8 fusion.13
  8.8 0.8 compare_select_fusion.2
  9.6 30.5 %scatter_custom_fusion = s32[8192]{0:T(1024)S(1)} fusion(s32[8192]{0:T(1024)S(1)} %compare_select_fusion.2, s32[8192]{0:T(1024)S(1)} %iota.68, s32[]{:T(128)} %constant.130.clone.1), kind=kCustom, calls=%fused_computation.84 | custom fusion | bytes 32772 | tf_op jit(solution)/shard_map/scatter | solution.py:67
  40.1 45.5 %gather_fusion = s32[8192]{0:T(1024)S(1)} fusion(s32[8192]{0:T(1024)S(1)} %get-tuple-element.16, s32[8192]{0:T(1024)S(1)} %maximum_clamp_fusion), kind=kCustom, calls=%fused_computation | custom fusion | bytes 98304 | tf_op jit(solution)/shard_map/jit(_take)/gather | solution.py:70
  85.6 0.6 select_select_fusion.1
  86.3 5.2 %all-to-all-start = ((s32[1,8,1024]{2,0,1:T(1,128)}), s32[1,8,1024]{2,0,1:T(1,128)S(1)}, u32[]{:S(2)}, u32[]{:S(2)}) async-start(s32[1,8,1024]{2,0,1:T(1,128)} %bitcast.4), calls=%async_computation | async-start | bytes 65536 | tf_op jit(solution)/shard_map/all_to_all | solution.py:73
  91.8 1.7 convolution_bitcast_fusion
  93.5 2.6 copy.9
  96.1 29.9 %gather_fusion.1 = f32[8192,16]{1,0:T(8,128)} fusion(f32[8192,16]{1,0:T(8,128)} %copy.9, s32[8192]{0:T(1024)S(1)} %maximum_clamp_fusion), kind=kCustom, calls=%fused_computation.1 | custom fusion | bytes 1081344 | tf_op jit(solution)/shard_map/jit(_take)/gather | solution.py:89
  126.0 2.8 copy.10
  129.0 2.7 collective-permute-start.6
  131.7 0.4 collective-permute-start.5
  132.0 1.3 collective-permute-start.4
  133.4 0.4 collective-permute-start.3
  134.0 30.5 %scatter_custom_fusion.1 = s32[4096]{0:T(1024)S(1)} fusion(s32[8192]{0:T(1024)S(1)} %bitcast.92, s32[8192]{0:T(1024)S(1)} %iota.69, s32[]{:T(128)} %constant.129.clone.1), kind=kCustom, calls=%fused_computation.93 | custom fusion | bytes 16388 | tf_op jit(solution)/shard_map/scatter | solution.py:77
  164.5 1.7 collective-permute-start.1
  166.3 2.7 collective-permute-done.1
  168.9 0.8 collective-permute-start.2
  169.8 3.4 %collective-permute-done.2 = f32[1024,16]{0,1:T(8,128)S(1)} collective-permute-done((f32[1024,16]{0,1:T(8,128)S(1)}, f32[1024,16]{0,1:T(8,128)S(1)}, u32[]{:S(2)}, u32[]{:S(2)}) %collective-permute-start.2) | collective-permute-done | bytes 65568 | tf_op jit(solution)/shard_map/ppermute | solution.py:96
  173.2 0.6 gather_fusion.2
  173.8 2.6 copy.11
  176.4 16.3 %gather_fusion.3 = f32[4096,16]{1,0:T(8,128)} fusion(f32[8192,16]{1,0:T(8,128)} %bitcast.86, s32[4096]{0:T(1024)S(1)} %fusion.27), kind=kCustom, calls=%fused_computation.3 | custom fusion | bytes 540672 | tf_op jit(solution)/shard_map/jit(_take)/gather | solution.py:99
  192.7 2.2 copy.12
  194.9 0.7 broadcast_select_fusion
  195.7 21.1 %reduce-scatter.5.cloned.1.call-done = f32[2,512,16]{1,2,0:T(8,128)} async-done(((f32[2,2048,16]{1,2,0:T(8,128)}), f32[2,512,16]{1,2,0:T(8,128)}) %reduce-scatter.5.cloned.1.call-update) | async-done | bytes 65552 | tf_op jit(solution)/shard_map/reduce_scatter | solution.py:101
  216.7 2.7 convolution_bitcast_fusion.1
  219.5 2.8 convolution_bitcast_fusion.2
  222.3 3.3 copy.13
  225.5 4.7 %reshape.303 = f32[1536,32]{1,0:T(8,128)} reshape(f32[1536,2,2,8]{3,2,1,0:T(2,128)} %bitcast.88) | data formatting | bytes 393216
  230.2 93.8 %reduce-scatter.7.cloned.1.call-done = f32[48,32]{1,0:T(8,128)} async-done(((f32[1536,32]{1,0:T(8,128)}), f32[48,32]{1,0:T(8,128)}) %reduce-scatter.7.cloned.1.call-update) | async-done | bytes 6160
  324.0 0.9 reshape.304
  324.9 0.7 copy.14
  (41 shorter events, 1.4 us)
Async XLA Ops:
  6.5 85.2 %copy-start = (bf16[8192,128]{1,0:T(8,128)(2,1)S(1)}, bf16[8192,128]{1,0:T(8,128)(2,1)}, u32[]{:S(2)}) copy-start(bf16[8192,128]{1,0:T(8,128)(2,1)} %param.4) | copy-start | bytes 6291460
  86.3 47.6 %all-to-all-start = ((s32[1,8,1024]{2,0,1:T(1,128)}), s32[1,8,1024]{2,0,1:T(1,128)S(1)}, u32[]{:S(2)}, u32[]{:S(2)}) async-start(s32[1,8,1024]{2,0,1:T(1,128)} %bitcast.4), calls=%async_computation | async-start | bytes 65536 | tf_op jit(solution)/shard_map/all_to_all | solution.py:73
  91.4 125.3 %reduce-scatter.5.cloned.1.call-start = ((), (), s32[]{:S(2)}) async-start(), calls=%async_computation.3 | async-start | bytes 327680 | tf_op jit(solution)/shard_map/reduce_scatter | solution.py:101
  129.0 44.2 %collective-permute-start.6 = (f32[1024,16]{0,1:T(8,128)S(1)}, f32[1024,16]{0,1:T(8,128)S(1)}, u32[]{:S(2)}, u32[]{:S(2)}) collective-permute-start(f32[1024,16]{0,1:T(8,128)S(1)} %get-tuple-element.8), channel_id=1, source_target_pairs={{0,28},{4,24},{8,20},{12,16},{16,12},{20,8},{24,4},{28,0},{1,29},{... | collective-permute-start | bytes 196616 | tf_op jit(solution)/shard_map/ppermute | solution.py:96
  131.7 41.5 %collective-permute-start.5 = (f32[1024,16]{0,1:T(8,128)S(1)}, f32[1024,16]{0,1:T(8,128)S(1)}, u32[]{:S(2)}, u32[]{:S(2)}) collective-permute-start(f32[1024,16]{0,1:T(8,128)S(1)} %get-tuple-element.9), channel_id=1, source_target_pairs={{0,24},{4,28},{8,16},{12,20},{16,8},{20,12},{24,0},{28,4},{1,25},{... | collective-permute-start | bytes 196616 | tf_op jit(solution)/shard_map/ppermute | solution.py:96
  132.0 41.1 %collective-permute-start.4 = (f32[1024,16]{0,1:T(8,128)S(1)}, f32[1024,16]{0,1:T(8,128)S(1)}, u32[]{:S(2)}, u32[]{:S(2)}) collective-permute-start(f32[1024,16]{0,1:T(8,128)S(1)} %get-tuple-element.10), channel_id=1, source_target_pairs={{0,20},{4,16},{8,28},{12,24},{16,4},{20,0},{24,12},{28,8},{1,21},{... | collective-permute-start | bytes 196616 | tf_op jit(solution)/shard_map/ppermute | solution.py:96
  133.4 39.7 %collective-permute-start.3 = (f32[1024,16]{0,1:T(8,128)S(1)}, f32[1024,16]{0,1:T(8,128)S(1)}, u32[]{:S(2)}, u32[]{:S(2)}) collective-permute-start(f32[1024,16]{0,1:T(8,128)S(1)} %get-tuple-element.11), channel_id=1, source_target_pairs={{0,16},{4,20},{8,24},{12,28},{16,0},{20,4},{24,8},{28,12},{1,17},{... | collective-permute-start | bytes 196616 | tf_op jit(solution)/shard_map/ppermute | solution.py:96
  133.7 30.8 %collective-permute-start = (f32[1024,16]{0,1:T(8,128)S(1)}, f32[1024,16]{0,1:T(8,128)S(1)}, u32[]{:S(2)}, u32[]{:S(2)}) collective-permute-start(f32[1024,16]{0,1:T(8,128)S(1)} %get-tuple-element.14), channel_id=1, source_target_pairs={{0,4},{4,0},{8,12},{12,8},{16,20},{20,16},{24,28},{28,24},{1,5},{5... | collective-permute-start | bytes 196616 | tf_op jit(solution)/shard_map/ppermute | solution.py:96
  164.5 4.4 %collective-permute-start.1 = (f32[1024,16]{0,1:T(8,128)S(1)}, f32[1024,16]{0,1:T(8,128)S(1)}, u32[]{:S(2)}, u32[]{:S(2)}) collective-permute-start(f32[1024,16]{0,1:T(8,128)S(1)} %get-tuple-element.13), channel_id=1, source_target_pairs={{0,8},{4,12},{8,0},{12,4},{16,24},{20,28},{24,16},{28,20},{1,9},{5... | collective-permute-start | bytes 196616 | tf_op jit(solution)/shard_map/ppermute | solution.py:96
  168.9 4.2 %collective-permute-start.2 = (f32[1024,16]{0,1:T(8,128)S(1)}, f32[1024,16]{0,1:T(8,128)S(1)}, u32[]{:S(2)}, u32[]{:S(2)}) collective-permute-start(f32[1024,16]{0,1:T(8,128)S(1)} %get-tuple-element.12), channel_id=1, source_target_pairs={{0,12},{4,8},{8,4},{12,0},{16,28},{20,24},{24,20},{28,16},{1,13},{... | collective-permute-start | bytes 196616 | tf_op jit(solution)/shard_map/ppermute | solution.py:96
  195.6 128.4 %reduce-scatter.7.cloned.1.call-start = ((), (), s32[]{:S(2)}) async-start(), calls=%async_computation.4 | async-start | bytes 811008
Sparse Core Ops, SparseCore 0:
  195.7 20.9 reduce-scatter.4
  230.3 93.6 reduce-scatter.6
